TPU v7x, 32 devices: a whole 2x2x4 slice. The times are simulated.
32 devices in a mesh: ctx: 8 (over y, x, core), head: 4 (over z).
Axes of the slice: x: 2, y: 2, z: 4, core: 2. Of those that a mesh axis runs over, the one named last changes fastest.
Arguments:
- routed_q: bfloat16 [4096, 1024], P('ctx', 'head'), may hold values from -16 to 16
- routed_k: bfloat16 [4096, 1024], P('ctx', 'head'), may hold values from -16 to 16
- routed_v: bfloat16 [4096, 1024], P('ctx', 'head'), may hold values from -6 to 6
- routed_grad: bfloat16 [4096, 1024], P('ctx', 'head'), may hold values from -6 to 6
- local_q: bfloat16 [4096, 1024], P('ctx', 'head'), may hold values from -16 to 16
- local_k: bfloat16 [4096, 1024], P('ctx', 'head'), may hold values from -16 to 16
- local_v: bfloat16 [4096, 1024], P('ctx', 'head'), may hold values from -6 to 6
- local_grad: bfloat16 [4096, 1024], P('ctx', 'head'), may hold values from -6 to 6
- clusters: int32 [8, 4096], P('head', 'ctx'), may hold values from 0 to 63, as said below
- cluster_slot: int32 [8, 64], P('head'), may hold values from 0 to 63, each once within a row
- rel_bias: float32 [128], replicated, may hold values from -4 to 4
Outputs:
- routed_out: bfloat16 [4096, 1024], P('ctx', 'head')
- routed_dq: bfloat16 [4096, 1024], P('ctx', 'head')
- routed_dk: bfloat16 [4096, 1024], P('ctx', 'head')
- routed_dv: bfloat16 [4096, 1024], P('ctx', 'head')
- centroids: float32 [8, 64, 128], P('head', 'ctx')
- local_out: bfloat16 [4096, 1024], P('ctx', 'head')
- local_dq: bfloat16 [4096, 1024], P('ctx', 'head')
- local_dk: bfloat16 [4096, 1024], P('ctx', 'head')
- local_dv: bfloat16 [4096, 1024], P('ctx', 'head')
- bias_grad: float32 [128], replicated
Inputs may be any that keep to these rules, and one draw needn't show every extreme that they name: `clusters`: among the 512 positions of one index of ctx, at most 16 name the same cluster for one routed head; for every routed head one cluster is named exactly 16 times on every index of ctx.
All inputs are finite; a program needn't handle non-finite values.
Results may differ from a plain program's by a relative error of at most 0.0077.
Values may be sent and summed in bfloat16 or wider, within the bound.
No kernel may reach another device: no remote copies, remote signals or barrier semaphores. Data moves between devices by JAX's collectives and lax.ppermute only.
A program may use at most 64 MiB of HBM per device.

v0:
```python
import jax
import jax.numpy as jnp
from jax import lax
from jax.sharding import PartitionSpec as P

HEAD_DIM = 128
WINDOW = 128
CLUSTER_MEAN = 64


NEG = -1e30
EPSILON = 1e-06


def from_behind(block, axis, distance):
    devices = range(lax.axis_size(axis))
    route = [(i - distance, i) for i in devices if i - distance in devices]
    return lax.ppermute(block, axis, route)


def softmax_rows(query, keys, allowed, offset_bias):
    scaling = query.shape[-1] ** (-0.5)
    scores = (
        jnp.einsum("bmd,bnd->bmn", query, keys, preferred_element_type=jnp.float32) * scaling
        + offset_bias
    )
    scores = jnp.where(allowed, scores, NEG)
    row_max = jnp.max(scores, axis=-1, keepdims=True)
    exponent = jnp.exp(scores - row_max)
    return exponent / jnp.sum(exponent, axis=-1, keepdims=True)


def weighted_values(weights_low, values):
    return jnp.einsum(
        "bmn,bnd->bmd", weights_low, values, preferred_element_type=jnp.float32
    ).astype(jnp.bfloat16)


def attention_grads(attn_weights, weights_low, query, keys, values, cotangent):
    weight_grad = jnp.einsum("bmd,bnd->bmn", cotangent, values, preferred_element_type=jnp.float32)
    score_grad = attn_weights * (
        weight_grad - jnp.sum(attn_weights * weight_grad, axis=-1, keepdims=True)
    )
    score_grad_low = score_grad.astype(jnp.bfloat16)
    scaling = query.shape[-1] ** (-0.5)
    query_grad = (
        jnp.einsum("bmn,bnd->bmd", score_grad_low, keys, preferred_element_type=jnp.float32)
        * scaling
    )
    keys_grad = (
        jnp.einsum("bmn,bmd->bnd", score_grad_low, query, preferred_element_type=jnp.float32)
        * scaling
    )
    values_grad = jnp.einsum(
        "bmn,bmd->bnd", weights_low, cotangent, preferred_element_type=jnp.float32
    )
    return (query_grad, keys_grad, values_grad, score_grad)


def plan_routes(cluster_ids, slots, ctx_size, per_source, per_dev):
    total = cluster_ids.shape[0]
    cluster_count = slots.shape[0]
    counts = jnp.sum(
        (cluster_ids[:, None] == jnp.arange(cluster_count, dtype=jnp.int32)[None, :]).astype(
            jnp.int32
        ),
        axis=0,
    )
    sorted_pos = jnp.argsort(cluster_ids, stable=True)
    sorted_ids = cluster_ids[sorted_pos]
    starts = jnp.cumsum(counts) - counts
    rank_in = jnp.arange(total, dtype=jnp.int32) - starts[sorted_ids]
    targets = slots[sorted_ids]
    flat_slot = (targets % per_dev * ctx_size + targets // per_dev) * per_source + rank_in
    destination = jnp.zeros((total,), jnp.int32).at[sorted_pos].set(flat_slot)
    filled = jnp.zeros((cluster_count,), jnp.int32).at[slots].set(counts).reshape(ctx_size, per_dev)
    return (destination, filled)


def offset_table():
    row_index = jnp.arange(WINDOW, dtype=jnp.int32)[:, None]
    col_index = jnp.arange(2 * WINDOW, dtype=jnp.int32)[None, :]
    offset = WINDOW + row_index - col_index
    inside = (offset >= 0) & (offset < WINDOW)
    return (offset, inside)


def shards(
    routed_q,
    routed_k,
    routed_v,
    routed_grad,
    local_q,
    local_k,
    local_v,
    local_grad,
    clusters,
    cluster_slot,
    rel_bias,
):
    ctx_size = lax.axis_size("ctx")
    tokens = routed_q.shape[0]
    head_dim = HEAD_DIM
    heads_here = routed_q.shape[1] // head_dim
    per_dev = tokens // CLUSTER_MEAN
    per_source = 2 * CLUSTER_MEAN // ctx_size
    capacity = per_source * ctx_size
    destination, filled = jax.vmap(
        lambda ids_row, slot_row: plan_routes(ids_row, slot_row, ctx_size, per_source, per_dev)
    )(clusters, cluster_slot)

    def split_heads(array, count):
        return array.reshape(tokens, count, head_dim).transpose(1, 0, 2)

    def packed(array):

        def one_head(token_rows, where_to):
            holder = (
                jnp.zeros((per_dev * ctx_size * per_source, head_dim), token_rows.dtype)
                .at[where_to]
                .set(token_rows)
            )
            return holder.reshape(per_dev, ctx_size, per_source, head_dim)

        return jax.vmap(one_head)(split_heads(array, heads_here), destination)

    def blocks(array):
        return array.reshape(heads_here * per_dev, capacity, head_dim)

    def unblock(array):
        return array.reshape(heads_here, per_dev, ctx_size, per_source, head_dim)

    def unpack(array):
        flat_rows = array.reshape(heads_here, per_dev * ctx_size * per_source, head_dim)
        token_rows = jax.vmap(lambda rows_head, where_to: rows_head[where_to])(
            flat_rows, destination
        )
        return token_rows.transpose(1, 0, 2).reshape(tokens, heads_here * head_dim)

    send_query = packed(routed_q)
    send_keys = packed(routed_k)
    send_values = packed(routed_v)
    send_cot = packed(routed_grad)
    got_counts = lax.all_to_all(filled, "ctx", split_axis=1, concat_axis=1, tiled=True)
    live_slots = (
        jnp.arange(per_source, dtype=jnp.int32)[None, None, None, :]
        < jnp.transpose(got_counts, (0, 2, 1))[..., None]
    ).reshape(heads_here * per_dev, capacity)
    causal = jnp.arange(capacity)[:, None] >= jnp.arange(capacity)[None, :]
    allowed = live_slots[:, None, :] & causal[None] | jnp.eye(capacity, dtype=bool)[None]
    local_count = local_q.shape[1] // head_dim
    block_count = tokens // WINDOW
    tail_keys, tail_values = from_behind((local_k[-WINDOW:], local_v[-WINDOW:]), "ctx", 1)

    def key_frames(earlier, array):
        extended = (
            jnp.concatenate([earlier, array], 0)
            .reshape(tokens + WINDOW, local_count, head_dim)
            .transpose(1, 0, 2)
        )
        return jnp.concatenate(
            [
                extended[:, :-WINDOW].reshape(local_count, block_count, WINDOW, head_dim),
                extended[:, WINDOW:].reshape(local_count, block_count, WINDOW, head_dim),
            ],
            2,
        ).reshape(local_count * block_count, 2 * WINDOW, head_dim)

    def query_blocks(array):
        return split_heads(array, local_count).reshape(local_count * block_count, WINDOW, head_dim)

    offset, inside = offset_table()
    offset_bias = jnp.take(rel_bias, jnp.clip(offset, 0, WINDOW - 1))
    key_pos = (
        lax.axis_index("ctx") * tokens
        + jnp.arange(block_count, dtype=jnp.int32)[:, None, None] * WINDOW
        - WINDOW
        + jnp.arange(2 * WINDOW, dtype=jnp.int32)[None, None, :]
    )
    window_allowed = jnp.broadcast_to(
        inside[None] & (key_pos >= 0), (local_count, block_count, WINDOW, 2 * WINDOW)
    )
    window_allowed = window_allowed.reshape(local_count * block_count, WINDOW, 2 * WINDOW)
    local_query = query_blocks(local_q)
    local_cot = query_blocks(local_grad)
    frame_keys = key_frames(tail_keys, local_k)
    frame_values = key_frames(tail_values, local_v)
    window_weights = softmax_rows(local_query, frame_keys, window_allowed, offset_bias)
    window_low = window_weights.astype(jnp.bfloat16)
    local_output = weighted_values(window_low, frame_values)
    local_qgrad, local_kgrad, local_vgrad, window_sgrad = attention_grads(
        window_weights, window_low, local_query, frame_keys, frame_values, local_cot
    )

    def fold_frames(array):
        array = array.reshape(local_count, block_count, 2 * WINDOW, head_dim)
        earlier_half = array[:, :, :WINDOW].reshape(local_count, tokens, head_dim)
        later_half = array[:, :, WINDOW:].reshape(local_count, tokens, head_dim)
        return jnp.pad(earlier_half, ((0, 0), (0, WINDOW), (0, 0))) + jnp.pad(
            later_half, ((0, 0), (WINDOW, 0), (0, 0))
        )

    keys_folded = fold_frames(local_kgrad)
    values_folded = fold_frames(local_vgrad)
    next_keys, next_values = (
        from_behind(keys_folded[:, :WINDOW].astype(jnp.bfloat16), "ctx", -1).astype(jnp.float32),
        from_behind(values_folded[:, :WINDOW].astype(jnp.bfloat16), "ctx", -1).astype(jnp.float32),
    )
    own_keys = keys_folded[:, WINDOW:].at[:, -WINDOW:].add(next_keys)
    own_values = values_folded[:, WINDOW:].at[:, -WINDOW:].add(next_values)

    def merge_local(array):
        return (
            array.reshape(local_count, tokens, head_dim)
            .transpose(1, 0, 2)
            .reshape(tokens, local_count * head_dim)
            .astype(jnp.bfloat16)
        )

    segment_ids = jnp.where(inside, offset, WINDOW).reshape(-1)
    score_total = jnp.sum(window_sgrad, axis=0)
    bias_part = jax.ops.segment_sum(score_total.reshape(-1), segment_ids, num_segments=WINDOW + 1)[
        :WINDOW
    ]
    bias_grad = lax.psum(bias_part, ("ctx", "head"))
    query_at, keys_at, values_at = (
        lax.all_to_all(send_query, "ctx", split_axis=2, concat_axis=2, tiled=True),
        lax.all_to_all(send_keys, "ctx", split_axis=2, concat_axis=2, tiled=True),
        lax.all_to_all(send_values, "ctx", split_axis=2, concat_axis=2, tiled=True),
    )
    owner_weights = softmax_rows(blocks(query_at), blocks(keys_at), allowed, 0.0)
    owner_low = owner_weights.astype(jnp.bfloat16)
    owner_output = weighted_values(owner_low, blocks(values_at))
    output_home = lax.all_to_all(
        unblock(owner_output), "ctx", split_axis=2, concat_axis=2, tiled=True
    )
    cot_at = lax.all_to_all(send_cot, "ctx", split_axis=2, concat_axis=2, tiled=True)
    owner_qgrad, owner_kgrad, owner_vgrad, unused = attention_grads(
        owner_weights,
        owner_low,
        blocks(query_at),
        blocks(keys_at),
        blocks(values_at),
        blocks(cot_at),
    )
    query_grad_home, keys_grad_home, values_grad_home = (
        lax.all_to_all(
            unblock(owner_qgrad.astype(jnp.bfloat16)),
            "ctx",
            split_axis=2,
            concat_axis=2,
            tiled=True,
        ),
        lax.all_to_all(
            unblock(owner_kgrad.astype(jnp.bfloat16)),
            "ctx",
            split_axis=2,
            concat_axis=2,
            tiled=True,
        ),
        lax.all_to_all(
            unblock(owner_vgrad.astype(jnp.bfloat16)),
            "ctx",
            split_axis=2,
            concat_axis=2,
            tiled=True,
        ),
    )
    key_sums = jnp.sum(blocks(keys_at), axis=1, dtype=jnp.float32)
    centroids = key_sums / jnp.sqrt(jnp.mean(key_sums * key_sums, axis=-1, keepdims=True) + EPSILON)
    centroids = centroids.reshape(heads_here, per_dev, head_dim)
    return (
        unpack(output_home),
        unpack(query_grad_home),
        unpack(keys_grad_home),
        unpack(values_grad_home),
        centroids,
        merge_local(local_output),
        merge_local(local_qgrad),
        merge_local(own_keys),
        merge_local(own_values),
        bias_grad,
    )


def solution(mesh):
    return jax.shard_map(
        shards,
        mesh=mesh,
        in_specs=(
            P("ctx", "head"),
            P("ctx", "head"),
            P("ctx", "head"),
            P("ctx", "head"),
            P("ctx", "head"),
            P("ctx", "head"),
            P("ctx", "head"),
            P("ctx", "head"),
            P("head", "ctx"),
            P("head", None),
            P(),
        ),
        out_specs=(
            P("ctx", "head"),
            P("ctx", "head"),
            P("ctx", "head"),
            P("ctx", "head"),
            P("head", "ctx", None),
            P("ctx", "head"),
            P("ctx", "head"),
            P("ctx", "head"),
            P("ctx", "head"),
            P(),
        ),
        check_vma=False,
    )
```

profile of v0, /device:TPU:0, one launch (start us, length us, event | category | flops | bytes accessed | tf_op | source)
XLA Modules:
  0.0 693.9 jit_solution(7077809286950077533)
XLA Ops:
  9.4 6.4 scatter_fusion
  16.5 5.2 all-to-all-start
  25.5 3.5 collective-permute-start.1
  34.2 193.9 %gather_fusion = f32[32768]{0:T(1024)S(1)} fusion(f32[128]{0:T(128)S(1)} %copy-done, s32[32768]{0:T(1024)S(1)} %broadcast_clamp_fusion), kind=kCustom, calls=%fused_computation | custom fusion | bytes 393216 | tf_op jit(solution)/shard_map/jit(_take)/gather | solution.py:173
  233.7 9.1 %gather_fusion.1 = s32[1024]{0:T(1024)S(1)} fusion(s32[2,512]{1,0:T(2,128)S(1)} %copy-done.2, s32[1024]{0:T(1024)S(1)} %bitcast.210), kind=kCustom, calls=%fused_computation.1 | custom fusion | bytes 16384 | tf_op jit(solution)/shard_map/vmap()/gather | solution.py:70
  242.8 9.0 %gather_fusion.2 = s32[1024]{0:T(1024)S(1)} fusion(s32[2,64]{1,0:T(2,128)S(1)} %copy-done.1, s32[1024]{0:T(1024)S(1)} %bitcast.208), kind=kCustom, calls=%fused_computation.2 | custom fusion | bytes 16384 | tf_op jit(solution)/shard_map/vmap()/gather | solution.py:73
  251.9 9.0 %gather_fusion.3 = s32[1024]{0:T(1024)S(1)} fusion(s32[2,64]{1,0:T(2,128)S(1)} %sub.111, s32[1024]{0:T(1024)S(1)} %bitcast.209), kind=kCustom, calls=%fused_computation.3 | custom fusion | bytes 16384 | tf_op jit(solution)/shard_map/vmap()/gather | solution.py:72
  261.0 4.3 scatter_custom_fusion.2
  275.2 3.7 all-to-all-start.1
  300.8 226.4 %scatter_custom_fusion = f32[129]{0:T(256)S(1)} fusion(s32[32768]{0:T(1024)} %bitcast.285, f32[32768]{0:T(1024)} %bitcast.286, f32[]{:T(128)} %constant.133.clone.1), kind=kCustom, calls=%fused_computation.155 | custom fusion | flops 32768 | bytes 1028 | tf_op jit(solution)/shard_map/scatter-add | solution.py:222
  527.3 42.6 %psum.7 = f32[128]{0:T(128)} all-reduce(f32[128]{0:T(128)S(1)} %slice.113), channel_id=1, replica_groups=mesh['ctx'=8,'head'=4] {'ctx','head'}, use_global_device_ids=true, to_apply=%region_19.20 | all-reduce | flops 128 | bytes 1024 | tf_op jit(solution)/shard_map/psum | solution.py:225
  572.0 4.6 all-to-all-start.2
  581.2 5.0 all-to-all-done.2
  586.3 4.4 all-to-all-start.3
  594.4 5.8 all-to-all-done.3
  613.3 4.1 all-to-all-start.4
  627.1 4.1 all-to-all-start.6
  634.6 6.4 all-to-all-done.6
  649.9 4.2 all-to-all-done.7
  654.2 3.5 all-to-all-start.8
  659.5 5.8 gather_fusion.4
  667.2 5.8 gather_fusion.5
  673.9 5.8 gather_fusion.6
  680.5 5.8 gather_fusion.7
  (220 shorter events, 100.2 us)
Async XLA Ops:
  7.2 27.0 %copy-start = (f32[128]{0:T(128)S(1)}, f32[128]{0:T(128)}, u32[]{:S(2)}) copy-start(f32[128]{0:T(128)} %param.25) | copy-start | bytes 1540
  7.2 224.3 %sort.19.cloned.1.call-start = ((), (), s32[]{:S(2)}) async-start(), calls=%async_computation.9 | async-start | bytes 24608 | tf_op jit(solution)/shard_map/vmap(jit(argsort))/sort | solution.py:69
  9.4 12.3 %copy-start.13 = (bf16[512,256]{1,0:T(8,128)(2,1)S(1)}, bf16[512,256]{1,0:T(8,128)(2,1)}, u32[]{:S(2)}) copy-start(bf16[512,256]{1,0:T(8,128)(2,1)} %param.20) | copy-start | bytes 786436
  9.4 15.5 %copy-start.14 = (bf16[512,256]{1,0:T(8,128)(2,1)S(1)}, bf16[512,256]{1,0:T(8,128)(2,1)}, u32[]{:S(2)}) copy-start(bf16[512,256]{1,0:T(8,128)(2,1)} %param.21) | copy-start | bytes 786436
  16.5 214.2 %all-to-all-start = ((s32[2,8,8]{2,0,1:T(2,128)}), s32[2,8,8]{2,0,1:T(2,128)S(1)}, u32[]{:S(2)}, u32[]{:S(2)}) async-start(s32[2,8,8]{2,0,1:T(2,128)} %copy.199), calls=%async_computation | async-start | bytes 16384 | tf_op jit(solution)/shard_map/all_to_all | solution.py:144
  22.3 7.9 %copy-start.16 = (bf16[512,256]{1,0:T(8,128)(2,1)S(1)}, bf16[512,256]{1,0:T(8,128)(2,1)}, u32[]{:S(2)}) copy-start(bf16[512,256]{1,0:T(8,128)(2,1)} %param.17) | copy-start | bytes 786436
  22.3 264.9 %collective-permute-start = (bf16[128,256]{1,0:T(8,128)(2,1)}, bf16[128,256]{1,0:T(8,128)(2,1)S(1)}, u32[]{:S(2)}, u32[]{:S(2)}) collective-permute-start(bf16[128,256]{1,0:T(8,128)(2,1)} %slice.97), channel_id=1, source_target_pairs={{0,4},{4,8},{8,12},{12,16},{16,20},{20,24},{24,28},{1,5},{5,9},{9,... | collective-permute-start | bytes 196616 | tf_op jit(solution)/shard_map/ppermute | solution.py:18
  25.5 261.9 %collective-permute-start.1 = (bf16[128,256]{1,0:T(8,128)(2,1)}, bf16[128,256]{1,0:T(8,128)(2,1)S(1)}, u32[]{:S(2)}, u32[]{:S(2)}) collective-permute-start(bf16[128,256]{1,0:T(8,128)(2,1)} %slice.100), channel_id=1, source_target_pairs={{0,4},{4,8},{8,12},{12,16},{16,20},{20,24},{24,28},{1,5},{5,9},{9,... | collective-permute-start | bytes 196616 | tf_op jit(solution)/shard_map/ppermute | solution.py:18
  230.5 58.4 %copy-start.24 = (f32[128,256]{0,1:T(8,128)}, f32[128,256]{0,1:T(8,128)S(1)}, u32[]{:S(2)}) copy-start(f32[128,256]{0,1:T(8,128)S(1)} %copy.238) | copy-start | bytes 393220
  275.2 296.8 %all-to-all-start.1 = ((bf16[2,8,8,16,128]{4,3,1,0,2:T(8,128)(2,1)}), bf16[2,8,8,16,128]{4,3,1,0,2:T(8,128)(2,1)S(1)}, u32[]{:S(2)}, u32[]{:S(2)}) async-start(bf16[2,8,8,16,128]{4,3,1,0,2:T(8,128)(2,1)} %copy.203), calls=%async_computation.1 | async-start | bytes 1048576 | tf_op jit(solution)/shard_map/all_to_all | solution.py:227
  287.3 1.6 copy-start.22
  293.8 2.4 copy-start.10
  294.9 336.4 %collective-permute-start.2 = (bf16[2,128,128]{2,0,1:T(2,128)(2,1)}, bf16[2,128,128]{2,0,1:T(2,128)(2,1)}, u32[]{:S(2)}, u32[]{:S(2)}) collective-permute-start(bf16[2,128,128]{2,0,1:T(2,128)(2,1)} %fusion.38), channel_id=1, source_target_pairs={{4,0},{8,4},{12,8},{16,12},{20,16},{24,20},{28,24},{5,1},{9,5},{13... | collective-permute-start | bytes 196616 | tf_op jit(solution)/shard_map/ppermute | solution.py:18
  297.8 346.8 %collective-permute-start.3 = (bf16[2,128,128]{2,0,1:T(2,128)(2,1)}, bf16[2,128,128]{2,0,1:T(2,128)(2,1)}, u32[]{:S(2)}, u32[]{:S(2)}) collective-permute-start(bf16[2,128,128]{2,0,1:T(2,128)(2,1)} %fusion.37), channel_id=1, source_target_pairs={{4,0},{8,4},{12,8},{16,12},{20,16},{24,20},{28,24},{5,1},{9,5},{13... | collective-permute-start | bytes 196616 | tf_op jit(solution)/shard_map/ppermute | solution.py:18
  572.0 14.3 %all-to-all-start.2 = ((bf16[2,8,8,16,128]{4,3,1,0,2:T(8,128)(2,1)}), bf16[2,8,8,16,128]{4,3,1,0,2:T(8,128)(2,1)S(1)}, u32[]{:S(2)}, u32[]{:S(2)}) async-start(bf16[2,8,8,16,128]{4,3,1,0,2:T(8,128)(2,1)} %copy.207), calls=%async_computation.2 | async-start | bytes 1048576 | tf_op jit(solution)/shard_map/all_to_all | solution.py:228
  586.3 13.9 %all-to-all-start.3 = ((bf16[2,8,8,16,128]{4,3,1,0,2:T(8,128)(2,1)}), bf16[2,8,8,16,128]{4,3,1,0,2:T(8,128)(2,1)}, u32[]{:S(2)}, u32[]{:S(2)}) async-start(bf16[2,8,8,16,128]{4,3,1,0,2:T(8,128)(2,1)} %copy.211), calls=%async_computation.3 | async-start | bytes 1048576 | tf_op jit(solution)/shard_map/all_to_all | solution.py:229
  600.1 13.1 %all-to-all-start.5 = ((bf16[2,8,8,16,128]{4,3,1,0,2:T(8,128)(2,1)}), bf16[2,8,8,16,128]{4,3,1,0,2:T(8,128)(2,1)S(1)}, u32[]{:S(2)}, u32[]{:S(2)}) async-start(bf16[2,8,8,16,128]{4,3,1,0,2:T(8,128)(2,1)} %copy.219), calls=%async_computation.5 | async-start | bytes 1048576 | tf_op jit(solution)/shard_map/all_to_all | solution.py:237
  603.6 2.0 copy-start.9
  613.3 13.9 %all-to-all-start.4 = ((bf16[2,8,8,16,128]{4,3,1,0,2:T(8,128)(2,1)}), bf16[2,8,8,16,128]{4,3,1,0,2:T(8,128)(2,1)}, u32[]{:S(2)}, u32[]{:S(2)}) async-start(bf16[2,8,8,16,128]{4,3,1,0,2:T(8,128)(2,1)} %copy.214), calls=%async_computation.4 | async-start | bytes 1048576 | tf_op jit(solution)/shard_map/all_to_all | solution.py:234
  617.5 2.9 copy-start.11
  627.1 13.9 %all-to-all-start.6 = ((bf16[2,8,8,16,128]{4,3,1,0,2:T(8,128)(2,1)}), bf16[2,8,8,16,128]{4,3,1,0,2:T(8,128)(2,1)}, u32[]{:S(2)}, u32[]{:S(2)}) async-start(bf16[2,8,8,16,128]{4,3,1,0,2:T(8,128)(2,1)} %copy.224), calls=%async_computation.6 | async-start | bytes 1048576 | tf_op jit(solution)/shard_map/all_to_all | solution.py:247
  631.3 1.6 copy-start.5
  641.0 13.1 %all-to-all-start.7 = ((bf16[2,8,8,16,128]{4,3,1,0,2:T(8,128)(2,1)}), bf16[2,8,8,16,128]{4,3,1,0,2:T(8,128)(2,1)S(1)}, u32[]{:S(2)}, u32[]{:S(2)}) async-start(bf16[2,8,8,16,128]{4,3,1,0,2:T(8,128)(2,1)} %copy.229), calls=%async_computation.7 | async-start | bytes 1048576 | tf_op jit(solution)/shard_map/all_to_all | solution.py:254
  654.2 26.3 %all-to-all-start.8 = ((bf16[2,8,8,16,128]{4,3,1,0,2:T(8,128)(2,1)}), bf16[2,8,8,16,128]{4,3,1,0,2:T(8,128)(2,1)S(1)}, u32[]{:S(2)}, u32[]{:S(2)}) async-start(bf16[2,8,8,16,128]{4,3,1,0,2:T(8,128)(2,1)} %copy.232), calls=%async_computation.8 | async-start | bytes 1048576 | tf_op jit(solution)/shard_map/all_to_all | solution.py:261
  (23 other events, 21.5 us)
Sparse Core Ops, SparseCore 0:
  11.0 2.8 sort.21.cloned.1.call-done
  (1 shorter events, 0.0 us)
where the time goes:
time: 696 us; the launch traced here: 694 us
  local copies, waits for them, and re-layouts  310 us (45%)
  other arithmetic  239 us (34%)
  starting transfers between devices  45.2 us (6%)
  blocking collectives  42.6 us (6%)
  waiting for transfers between devices  23.6 us (3%)
  matrix products  18.4 us (3%)
  between operations  15 us (2%)
    scatter-add x1, other arithmetic, shards(): jax.ops.segment_sum(score_total.reshape(-1), segment_ids, num_segments=WI...  226 us
    gather x2, local copies, waits for them, and re-layouts, shards(): offset_bias = jnp.take(rel_bias, jnp.clip(offset, 0, WINDOW - 1))  194 us
    psum x1, blocking collectives, shards(): bias_grad = lax.psum(bias_part, ('ctx', 'head'))  42.6 us
    unnamed x87, local copies, waits for them, and re-layouts  30.6 us
    gather x4, local copies, waits for them, and re-layouts, unpack(): rows_head[where_to]  23.3 us
  transfers between devices with their start and end apart: 13, of which 6 were waited for; matrix products, arithmetic and copies ran while one was open for 78% of the time, Pallas kernels for 0%

commit v1 on v0

v1 whole, which is shorter than its diff:
```python
import jax
import jax.numpy as jnp
from jax import lax
from jax.experimental import pallas as pl
from jax.experimental.pallas import tpu as pltpu
from jax.sharding import PartitionSpec as P

HEAD_DIM = 128
WINDOW = 128

NEG = -1e30
EPSILON = 1e-06
EMPTY = 64.0
EMPTY_LEVEL = 32.0

F32 = jnp.float32
BF16 = jnp.bfloat16


def dot_nn(a, b):
    return lax.dot_general(a, b, (((1,), (0,)), ((), ())), preferred_element_type=F32)


def dot_nt(a, b):
    return lax.dot_general(a, b, (((1,), (1,)), ((), ())), preferred_element_type=F32)


def dot_tn(a, b):
    return lax.dot_general(a, b, (((0,), (0,)), ((), ())), preferred_element_type=F32)


def iota(shape, dim):
    return lax.broadcasted_iota(jnp.int32, shape, dim)


def softmax_and_grads(query, keys, values, cotangent, bias, allowed):
    scaling = query.shape[-1] ** (-0.5)
    scores = dot_nt(query, keys) * scaling
    if bias is not None:
        scores = scores + bias
    scores = jnp.where(allowed, scores, NEG)
    exponent = jnp.exp(scores - jnp.max(scores, axis=-1, keepdims=True))
    probs = exponent * (1.0 / jnp.sum(exponent, axis=-1, keepdims=True))
    dprobs = dot_nt(cotangent, values)
    dscores = probs * (dprobs - jnp.sum(probs * dprobs, axis=-1, keepdims=True))
    return probs, dscores


def pack_kernel(ids_ref, slots_ref, q_ref, k_ref, v_ref, g_ref, out_ref, flat_ref, *, per_source):
    head = pl.program_id(0)
    ids = ids_ref[pl.ds(head, 1), :]
    tokens = ids.shape[1]
    clusters = slots_ref.shape[1]
    dests, _, rows, _ = out_ref.shape
    member = iota((clusters, tokens), 0) == ids
    member_low = jnp.where(member, 1.0, 0.0).astype(BF16)
    earlier = jnp.where(iota((tokens, tokens), 0) < iota((tokens, tokens), 1), 1.0, 0.0).astype(BF16)
    before = dot_nn(member_low, earlier)
    rank = jnp.sum(jnp.where(member, before, 0.0), axis=0, keepdims=True)
    slots = jnp.broadcast_to(slots_ref[pl.ds(head, 1), :], (8, clusters)).astype(F32).astype(BF16)
    flat = dot_nn(slots, member_low)[:1] * per_source + rank
    flat_ref[0] = jnp.broadcast_to(flat, (8, tokens))
    where_to = flat.astype(jnp.int32)
    data = jnp.concatenate([q_ref[...], k_ref[...], v_ref[...], g_ref[...]], axis=1)
    dim = k_ref.shape[1]
    first_col = iota((rows, dim), 1) == 0
    for dest in range(dests):
        chosen = jnp.where(iota((rows, tokens), 0) + dest * rows == where_to, 1.0, 0.0)
        filled = jnp.sum(chosen, axis=1, keepdims=True) > 0.5
        moved = dot_nn(chosen.astype(BF16), data)
        marked = jnp.where(first_col & ~filled, EMPTY, moved[:, dim : 2 * dim])
        out_ref[dest, 0, :, :dim] = moved[:, :dim].astype(BF16)
        out_ref[dest, 0, :, dim : 2 * dim] = marked.astype(BF16)
        out_ref[dest, 0, :, 2 * dim :] = moved[:, 2 * dim :].astype(BF16)


def pack(ids, slots, arrays, dests, per_source):
    tokens = arrays[0].shape[0]
    heads, clusters = slots.shape
    rows = clusters * per_source // dests
    width = len(arrays) * HEAD_DIM
    column = pl.BlockSpec((tokens, HEAD_DIM), lambda h: (0, h))
    return pl.pallas_call(
        lambda *refs: pack_kernel(*refs, per_source=per_source),
        grid=(heads,),
        in_specs=[
            pl.BlockSpec((heads, tokens), lambda h: (0, 0)),
            pl.BlockSpec((heads, clusters), lambda h: (0, 0)),
            column,
            column,
            column,
            column,
        ],
        out_specs=(
            pl.BlockSpec((dests, 1, rows, width), lambda h: (0, h, 0, 0)),
            pl.BlockSpec((1, 8, tokens), lambda h: (h, 0, 0)),
        ),
        out_shape=(
            jax.ShapeDtypeStruct((dests, heads, rows, width), BF16),
            jax.ShapeDtypeStruct((heads, 8, tokens), F32),
        ),
        name="pack",
    )(ids, slots, *arrays)


def owner_kernel(got_ref, out_ref, centroid_ref, *, per_source):
    sources, _, rows, _ = got_ref.shape
    dim = HEAD_DIM
    capacity = sources * per_source
    row = iota((capacity, capacity), 0)
    col = iota((capacity, capacity), 1)
    causal = row >= col
    diagonal = row == col
    pick_first = jnp.where(iota((capacity, dim), 1) == 0, 1.0, 0.0).astype(BF16)
    first_col = iota((capacity, dim), 1) == 0
    scaling = dim ** (-0.5)
    sums = []
    for cluster in range(rows // per_source):
        at = slice(cluster * per_source, (cluster + 1) * per_source)
        block = jnp.concatenate([got_ref[s, 0, at, :] for s in range(sources)], axis=0)
        query = block[:, :dim]
        keys = block[:, dim : 2 * dim]
        values = block[:, 2 * dim : 3 * dim]
        cotangent = block[:, 3 * dim :]
        live = dot_nt(pick_first, keys) < EMPTY_LEVEL
        allowed = (live & causal) | diagonal
        probs, dscores = softmax_and_grads(query, keys, values, cotangent, None, allowed)
        probs_low = probs.astype(BF16)
        dscores_low = dscores.astype(BF16)
        result = jnp.concatenate(
            [
                dot_nn(probs_low, values).astype(BF16),
                (dot_nn(dscores_low, keys) * scaling).astype(BF16),
                (dot_tn(dscores_low, query) * scaling).astype(BF16),
                dot_tn(probs_low, cotangent).astype(BF16),
            ],
            axis=1,
        )
        for s in range(sources):
            out_ref[s, 0, at, :] = result[s * per_source : (s + 1) * per_source]
        wide = keys.astype(F32)
        sums.append(jnp.sum(jnp.where(first_col & (wide > EMPTY_LEVEL), 0.0, wide), axis=0, keepdims=True))
    key_sums = jnp.concatenate(sums, axis=0)
    norm = jnp.sqrt(jnp.mean(key_sums * key_sums, axis=-1, keepdims=True) + EPSILON)
    centroid_ref[0] = key_sums / norm


def owner(got, per_source):
    sources, heads, rows, width = got.shape
    block = pl.BlockSpec((sources, 1, rows, width), lambda h: (0, h, 0, 0))
    held = rows // per_source
    return pl.pallas_call(
        lambda *refs: owner_kernel(*refs, per_source=per_source),
        grid=(heads,),
        in_specs=[block],
        out_specs=(block, pl.BlockSpec((1, held, HEAD_DIM), lambda h: (h, 0, 0))),
        out_shape=(
            jax.ShapeDtypeStruct(got.shape, BF16),
            jax.ShapeDtypeStruct((heads, held, HEAD_DIM), F32),
        ),
        name="owner",
    )(got)


def unpack_kernel(flat_ref, home_ref, *out_refs):
    tokens = flat_ref.shape[2]
    sources, _, rows, width = home_ref.shape
    lanes = HEAD_DIM
    wide = jnp.broadcast_to(flat_ref[0, :1, :], (lanes, tokens)).T.astype(jnp.int32)
    lane = iota((tokens, lanes), 1)
    slots = sources * rows
    chosen = jnp.concatenate(
        [jnp.where(wide == lane + at, 1.0, 0.0).astype(BF16) for at in range(0, slots, lanes)], axis=1
    )
    moved = dot_nn(chosen, home_ref[:, 0].reshape(slots, width)).astype(BF16)
    for n, out_ref in enumerate(out_refs):
        out_ref[...] = moved[:, n * HEAD_DIM : (n + 1) * HEAD_DIM]


def unpack(flat, home):
    heads, _, tokens = flat.shape
    sources, _, rows, width = home.shape
    outs = width // HEAD_DIM
    column = pl.BlockSpec((tokens, HEAD_DIM), lambda h: (0, h))
    return pl.pallas_call(
        unpack_kernel,
        grid=(heads,),
        in_specs=[
            pl.BlockSpec((1, 8, tokens), lambda h: (h, 0, 0)),
            pl.BlockSpec((sources, 1, rows, width), lambda h: (0, h, 0, 0)),
        ],
        out_specs=(column,) * outs,
        out_shape=(jax.ShapeDtypeStruct((tokens, heads * HEAD_DIM), BF16),) * outs,
        name="unpack",
    )(flat, home)


def shift_rows(array, sign):
    count, lanes = array.shape
    row = iota((count, lanes), 0)
    step = 1
    while step < count:
        rolled = pltpu.roll(array, step if sign > 0 else lanes - step, 1)
        array = jnp.where((row // step) % 2 == 1, rolled, array)
        step *= 2
    return array


def local_kernel(
    first_ref,
    bias_ref,
    q_ref,
    k_ref,
    v_ref,
    g_ref,
    pk_ref,
    pv_ref,
    nq_ref,
    nk_ref,
    nv_ref,
    ng_ref,
    out_ref,
    dq_ref,
    dk_ref,
    dv_ref,
    part_ref,
):
    tokens, dim = q_ref.shape
    scaling = dim ** (-0.5)
    size = (WINDOW, 2 * WINDOW)
    row = iota(size, 0)
    col = iota(size, 1)
    inside = (col > row) & (col <= row + WINDOW)
    inside_first = inside & (col >= WINDOW * first_ref[0, 0])
    bias = shift_rows(jnp.broadcast_to(bias_ref[...], size), 1)
    count = tokens // WINDOW
    total = jnp.zeros(size, F32)
    late_dk = late_dv = None
    for b in range(count + 1):
        at = slice(b * WINDOW, (b + 1) * WINDOW)
        if b < count:
            query, late_k, late_v, cot = q_ref[at], k_ref[at], v_ref[at], g_ref[at]
        else:
            query, late_k, late_v, cot = nq_ref[...], nk_ref[...], nv_ref[...], ng_ref[...]
        behind = slice((b - 1) * WINDOW, b * WINDOW)
        early_k = pk_ref[...] if b == 0 else k_ref[behind]
        early_v = pv_ref[...] if b == 0 else v_ref[behind]
        keys = jnp.concatenate([early_k, late_k], axis=0)
        values = jnp.concatenate([early_v, late_v], axis=0)
        probs, dscores = softmax_and_grads(
            query, keys, values, cot, bias, inside_first if b == 0 else inside
        )
        probs_low = probs.astype(BF16)
        dscores_low = dscores.astype(BF16)
        if b < count:
            total = total + dscores
            out_ref[at] = dot_nn(probs_low, values).astype(BF16)
            dq_ref[at] = (dot_nn(dscores_low, keys) * scaling).astype(BF16)
        if b > 0:
            early_dk = dot_tn(dscores_low[:, :WINDOW], query)
            early_dv = dot_tn(probs_low[:, :WINDOW], cot)
            dk_ref[behind] = ((late_dk + early_dk) * scaling).astype(BF16)
            dv_ref[behind] = (late_dv + early_dv).astype(BF16)
        if b < count:
            late_dk = dot_tn(dscores_low[:, WINDOW:], query)
            late_dv = dot_tn(probs_low[:, WINDOW:], cot)
    part = jnp.sum(shift_rows(total, -1), axis=0, keepdims=True)
    part = jnp.broadcast_to(part, part_ref.shape)

    @pl.when(pl.program_id(0) == 0)
    def _():
        part_ref[...] = part

    @pl.when(pl.program_id(0) > 0)
    def _():
        part_ref[...] += part


def local(first, bias_row, own, behind, ahead, copies):
    tokens, columns = own[0].shape
    heads = columns // HEAD_DIM
    column = pl.BlockSpec((tokens, HEAD_DIM), lambda h: (0, h))

    def halo(n):
        return pl.BlockSpec((WINDOW, HEAD_DIM), lambda h: (0, n * heads + h))

    return pl.pallas_call(
        local_kernel,
        grid=(heads,),
        in_specs=[
            pl.BlockSpec((1, 1), lambda h: (0, 0), memory_space=pltpu.SMEM),
            pl.BlockSpec((1, 2 * WINDOW), lambda h: (0, 0)),
            column,
            column,
            column,
            column,
            halo(0),
            halo(1),
            halo(0),
            halo(1),
            halo(2),
            halo(3),
        ],
        out_specs=(column,) * 4 + (pl.BlockSpec((copies, 2 * WINDOW), lambda h: (0, 0)),),
        out_shape=(jax.ShapeDtypeStruct((tokens, columns), BF16),) * 4
        + (jax.ShapeDtypeStruct((copies, 2 * WINDOW), F32),),
        name="local",
    )(first, bias_row, *own, behind, behind, ahead, ahead, ahead, ahead)


def shards(
    routed_q,
    routed_k,
    routed_v,
    routed_grad,
    local_q,
    local_k,
    local_v,
    local_grad,
    clusters,
    cluster_slot,
    rel_bias,
):
    ctx_size = lax.axis_size("ctx")
    device_count = ctx_size * lax.axis_size("head")
    tokens = routed_q.shape[0]
    per_source = 2 * tokens // cluster_slot.shape[1]

    sent, flat = pack(
        clusters, cluster_slot, (routed_q, routed_k, routed_v, routed_grad), ctx_size, per_source
    )
    got = lax.all_to_all(sent, "ctx", 0, 0, tiled=True)

    tail = jnp.concatenate([local_k[-WINDOW:], local_v[-WINDOW:]], axis=1)
    lead = jnp.concatenate([a[:WINDOW] for a in (local_q, local_k, local_v, local_grad)], axis=1)
    behind = lax.ppermute(tail, "ctx", [(i, i + 1) for i in range(ctx_size - 1)])
    ahead = lax.ppermute(lead, "ctx", [(i + 1, i) for i in range(ctx_size - 1)])
    first = (lax.axis_index("ctx") == 0).astype(jnp.int32).reshape(1, 1)
    bias_row = jnp.concatenate(
        [jnp.zeros((1,), F32), rel_bias[::-1], jnp.zeros((WINDOW - 1,), F32)]
    ).reshape(1, 2 * WINDOW)
    local_out, local_dq, local_dk, local_dv, part = local(
        first, bias_row, (local_q, local_k, local_v, local_grad), behind, ahead, device_count
    )
    parts = lax.all_to_all(part, ("ctx", "head"), 0, 0, tiled=True)
    bias_grad = jnp.sum(parts, axis=0)[1 : WINDOW + 1][::-1]

    back, centroids = owner(got, per_source)
    home = lax.all_to_all(back, "ctx", 0, 0, tiled=True)
    routed_out, routed_dq, routed_dk, routed_dv = unpack(flat, home)
    return (
        routed_out,
        routed_dq,
        routed_dk,
        routed_dv,
        centroids,
        local_out,
        local_dq,
        local_dk,
        local_dv,
        bias_grad,
    )


def solution(mesh):
    return jax.shard_map(
        shards,
        mesh=mesh,
        in_specs=(
            P("ctx", "head"),
            P("ctx", "head"),
            P("ctx", "head"),
            P("ctx", "head"),
            P("ctx", "head"),
            P("ctx", "head"),
            P("ctx", "head"),
            P("ctx", "head"),
            P("head", "ctx"),
            P("head", None),
            P(),
        ),
        out_specs=(
            P("ctx", "head"),
            P("ctx", "head"),
            P("ctx", "head"),
            P("ctx", "head"),
            P("head", "ctx", None),
            P("ctx", "head"),
            P("ctx", "head"),
            P("ctx", "head"),
            P("ctx", "head"),
            P(),
        ),
        check_vma=False,
    )
```

time: 696 us -> 100 us (0.14)
  local copies, waits for them, and re-layouts: 310 us -> 4.31 us
  other arithmetic: 239 us -> 0.73 us
  blocking collectives: 42.6 us -> 0 us
  Pallas kernels: 0 us -> 25.6 us
  matrix products: 18.4 us -> 0 us
  between operations: 15 us -> 0.8 us
  starting transfers between devices: 45.2 us -> 31.4 us
  waiting for transfers between devices: 23.6 us -> 37.1 us
    gather x12 -> x0, local copies, waits for them, and re-layouts: 244 us -> none  [the longest x2 194 us: shards(): offset_bias = jnp.take(rel_bias, jnp.clip(offset, 0, WINDOW - 1))]
    scatter-add x3 -> x0, other arithmetic: 229 us -> none  [the longest x1 226 us: shards(): jax.ops.segment_sum(score_total.reshape(-1), segment_ids, num_segments=WI...]
    psum x1 -> x0, blocking collectives: 42.6 us -> none  [shards(): bias_grad = lax.psum(bias_part, ('ctx', 'head'))]
    unnamed x87 -> x14, local copies, waits for them, and re-layouts: 30.6 us -> 2.09 us
    pallas_call x0 -> x4, Pallas kernels: none -> 25.6 us  [the longest x1 9.91 us: owner(): pl.pallas_call(lambda *refs: owner_kernel(*refs, per_source=per_source),...]
    dot_general x11 -> x0, matrix products: 17.9 us -> none  [the longest x2 5.73 us: weighted_values(): jnp.einsum('bmn,bnd->bmd', weights_low, values, preferred_element_type=jn...]
    reshape x20 -> x0, local copies, waits for them, and re-layouts: 14.4 us -> none  [the longest x4 5.51 us: unblock(): return array.reshape(heads_here, per_dev, ctx_size, per_source, head_dim)]
    all_to_all x9 -> x3, waiting for transfers between devices: 23.6 us -> 36.9 us  [the longest x1 25.9 us: shards(): home = lax.all_to_all(back, 'ctx', 0, 0, tiled=True)]
  transfers between devices with their start and end apart: 13 -> 5, of which waited for: 6 -> 3; matrix products, arithmetic and copies ran while one was open for 78% -> 3% of each run, Pallas kernels for 0% -> 18%
where the time goes in v1:
time: 100 us
  waiting for transfers between devices  37.1 us (37%)
  starting transfers between devices  31.4 us (31%)
  Pallas kernels  25.6 us (26%)
  local copies, waits for them, and re-layouts  4.31 us (4%)
    all_to_all x1, waiting for transfers between devices, shards(): home = lax.all_to_all(back, 'ctx', 0, 0, tiled=True)  25.9 us
    all_to_all x1, starting transfers between devices, shards(): parts = lax.all_to_all(part, ('ctx', 'head'), 0, 0, tiled=True)  17.8 us
    all_to_all x1, waiting for transfers between devices, shards(): got = lax.all_to_all(sent, 'ctx', 0, 0, tiled=True)  11 us
    pallas_call x1, Pallas kernels, owner(): pl.pallas_call(lambda *refs: owner_kernel(*refs, per_source=per_source),...  9.91 us
    pallas_call x1, Pallas kernels, local(): pl.pallas_call(local_kernel, grid=(heads,), in_specs=[pl.BlockSpec((1, 1)...  8.02 us
    all_to_all x1, starting transfers between devices, shards(): got = lax.all_to_all(sent, 'ctx', 0, 0, tiled=True)  5.32 us
    pallas_call x1, Pallas kernels, pack(): pl.pallas_call(lambda *refs: pack_kernel(*refs, per_source=per_source), g...  4.11 us
    all_to_all x1, starting transfers between devices, shards(): home = lax.all_to_all(back, 'ctx', 0, 0, tiled=True)  3.95 us
  transfers between devices with their start and end apart: 5, of which 3 were waited for; matrix products, arithmetic and copies ran while one was open for 3% of the time, Pallas kernels for 18%

profile of v1, /device:TPU:0, one launch (start us, length us, event | category | flops | bytes accessed | tf_op | source)
XLA Modules:
  0.0 100.0 jit_solution(6719716616986459379)
XLA Ops:
  0.6 4.1 %pack.1 = (bf16[8,2,128,512]{3,2,1,0:T(8,128)(2,1)}, f32[2,8,512]{2,1,0:T(8,128)}) custom-call(s32[2,512]{1,0:T(2,128)} %refs_0_.1, s32[2,64]{1,0:T(2,128)} %refs_1_.1, bf16[512,256]{1,0:T(8,128)(2,1)} %refs_2_.1, bf16[512,256]{1,0:T(8,128)(2,1)} %refs_3_.1, bf16[512,256]{1,0:T(8,128)(2,1)} %refs_4_.1, bf16[512,256]{1,0:T(8,128)(2,1)} %refs_5_.1), custom_call_target="tpu_custom_call" | custom-call | tf_op jit(solution)/shard_map/pack/pallas_call | solution.py:83
  4.8 0.0 copy-start.4
  4.8 0.0 slice-start
  4.8 0.0 slice-start.1
  4.8 5.3 %all-to-all-start = ((bf16[8,2,128,512]{3,2,1,0:T(8,128)(2,1)}), bf16[8,2,128,512]{3,2,1,0:T(8,128)(2,1)S(1)}, u32[]{:S(2)}, u32[]{:S(2)}) async-start(bf16[8,2,128,512]{3,2,1,0:T(8,128)(2,1)} %get-tuple-element.24), calls=%async_computation | async-start | bytes 4194304 | tf_op jit(solution)/shard_map/all_to_all | solution.py:332
  10.2 1.3 %collective-permute-start.1 = (bf16[128,1024]{1,0:T(8,128)(2,1)S(1)}, bf16[128,1024]{1,0:T(8,128)(2,1)S(1)}, u32[]{:S(2)}, u32[]{:S(2)}) collective-permute-start(bf16[128,1024]{1,0:T(8,128)(2,1)S(1)} %pad_maximum_fusion), channel_id=1, source_target_pairs={{4,0},{8,4},{12,8},{16,12},{20,16},{24,20},{28,24},{5,1},{9,5},{13... | collective-permute-start | bytes 786440 | tf_op jit(solution)/shard_map/ppermute | solution.py:337
  11.5 3.0 %collective-permute-start = (bf16[128,512]{1,0:T(8,128)(2,1)S(1)}, bf16[128,512]{1,0:T(8,128)(2,1)S(1)}, u32[]{:S(2)}, u32[]{:S(2)}) collective-permute-start(bf16[128,512]{1,0:T(8,128)(2,1)S(1)} %pad_maximum_fusion.1), channel_id=1, source_target_pairs={{0,4},{4,8},{8,12},{12,16},{16,20},{20,24},{24,28},{1,5},{5,9},{9,... | collective-permute-start | bytes 393224 | tf_op jit(solution)/shard_map/ppermute | solution.py:336
  14.6 0.1 rev.6
  14.7 0.6 pad_maximum_fusion.2
  15.3 0.2 collective-permute-done.pk_ref.pv_ref
  15.6 0.6 copy-done.5
  16.2 0.1 copy-done.2
  16.3 8.0 %local.1 = (bf16[512,256]{1,0:T(8,128)(2,1)}, bf16[512,256]{1,0:T(8,128)(2,1)}, bf16[512,256]{1,0:T(8,128)(2,1)}, bf16[512,256]{1,0:T(8,128)(2,1)}, f32[32,256]{1,0:T(8,128)}) custom-call(s32[1,1]{1,0:T(1,128)} %bitcast.first_ref, f32[1,256]{1,0:T(1,128)} %bitcast.4, bf16[512,256]{1,0:T(8,128)(2,1)} %q_ref.1, bf16[512,256]{1,0:T(8,128)(2,1)} %k_ref.1, ...), custom_call_target="tpu_custom_call" | custom-call | tf_op jit(solution)/shard_map/local/pallas_call | solution.py:287
  24.3 1.4 %copy.21 = f32[32,1,256]{2,1,0:T(1,128)} copy(f32[32,1,256]{2,0,1:T(8,128)} %bitcast.3) | data formatting | bytes 65536 | tf_op jit(solution)/shard_map/all_to_all | solution.py:345
  25.7 11.0 %all-to-all-done.refs_0_ = bf16[8,2,128,512]{3,2,1,0:T(8,128)(2,1)S(1)} async-done(((bf16[8,2,128,512]{3,2,1,0:T(8,128)(2,1)}), bf16[8,2,128,512]{3,2,1,0:T(8,128)(2,1)S(1)}, u32[]{:S(2)}, u32[]{:S(2)}) %all-to-all-start) | async-done | bytes 2097184 | tf_op jit(solution)/shard_map/all_to_all | solution.py:332
  36.7 17.8 %all-to-all-start.2 = ((f32[32,1,256]{2,1,0:T(1,128)}), f32[32,1,256]{2,1,0:T(1,128)S(1)}, u32[]{:S(2)}, u32[]{:S(2)}) async-start(f32[32,1,256]{2,1,0:T(1,128)} %copy.21), calls=%async_computation.2 | async-start | bytes 65536 | tf_op jit(solution)/shard_map/all_to_all | solution.py:345
  54.6 9.9 %owner.1 = (bf16[8,2,128,512]{3,2,1,0:T(8,128)(2,1)}, f32[2,8,128]{2,1,0:T(8,128)}) custom-call(bf16[8,2,128,512]{3,2,1,0:T(8,128)(2,1)} %copy-done), custom_call_target="tpu_custom_call" | custom-call | tf_op jit(solution)/shard_map/owner/pallas_call | solution.py:152
  64.5 3.9 %all-to-all-start.1 = ((bf16[8,2,128,512]{3,2,1,0:T(8,128)(2,1)}), bf16[8,2,128,512]{3,2,1,0:T(8,128)(2,1)S(1)}, u32[]{:S(2)}, u32[]{:S(2)}) async-start(bf16[8,2,128,512]{3,2,1,0:T(8,128)(2,1)} %get-tuple-element.25), calls=%async_computation.1 | async-start | bytes 4194304 | tf_op jit(solution)/shard_map/all_to_all | solution.py:349
  68.4 0.1 reduce_sum.9
  68.5 0.1 slice.27
  68.6 0.6 rev.7
  69.2 25.9 %all-to-all-done.1.home_ref = bf16[8,2,128,512]{3,2,1,0:T(8,128)(2,1)S(1)} async-done(((bf16[8,2,128,512]{3,2,1,0:T(8,128)(2,1)}), bf16[8,2,128,512]{3,2,1,0:T(8,128)(2,1)S(1)}, u32[]{:S(2)}, u32[]{:S(2)}) %all-to-all-start.1) | async-done | bytes 2097184 | tf_op jit(solution)/shard_map/all_to_all | solution.py:349
  95.0 1.3 %copy-done.1 = bf16[8,2,128,512]{3,2,1,0:T(8,128)(2,1)} copy-done((bf16[8,2,128,512]{3,2,1,0:T(8,128)(2,1)}, bf16[8,2,128,512]{3,2,1,0:T(8,128)(2,1)S(1)}, u32[]{:S(2)}) %copy-start.1) | copy-done | bytes 2097176
  96.4 3.6 %unpack.1 = (bf16[512,256]{1,0:T(8,128)(2,1)}, bf16[512,256]{1,0:T(8,128)(2,1)}, bf16[512,256]{1,0:T(8,128)(2,1)}, bf16[512,256]{1,0:T(8,128)(2,1)}) custom-call(f32[2,8,512]{2,1,0:T(8,128)} %get-tuple-element.23.flat_ref, bf16[8,2,128,512]{3,2,1,0:T(8,128)(2,1)} %copy-done.1), custom_call_target="tpu_custom_call" | custom-call | tf_op jit(solution)/shard_map/unpack/pallas_call | solution.py:185
  (18 shorter events, 0.1 us)
Async XLA Ops:
  4.8 5.4 %copy-start.3 = (bf16[512,256]{1,0:T(8,128)(2,1)S(1)}, bf16[512,256]{1,0:T(8,128)(2,1)}, u32[]{:S(2)}) copy-start(bf16[512,256]{1,0:T(8,128)(2,1)} %k_ref.1) | copy-start | bytes 786436
  4.8 5.4 %copy-start.4 = (bf16[512,256]{1,0:T(8,128)(2,1)S(1)}, bf16[512,256]{1,0:T(8,128)(2,1)}, u32[]{:S(2)}) copy-start(bf16[512,256]{1,0:T(8,128)(2,1)} %v_ref.1) | copy-start | bytes 786436
  4.8 5.4 %slice-start = ((bf16[512,256]{1,0:T(8,128)(2,1)}), bf16[128,256]{1,0:T(8,128)(2,1)S(1)}, s32[]{:S(2)}) async-start(bf16[512,256]{1,0:T(8,128)(2,1)} %q_ref.1), calls=%async_computation.3 | async-start | bytes 131072 | tf_op jit(solution)/shard_map/slice | solution.py:335
  4.8 5.4 %slice-start.1 = ((bf16[512,256]{1,0:T(8,128)(2,1)}), bf16[128,256]{1,0:T(8,128)(2,1)S(1)}, s32[]{:S(2)}) async-start(bf16[512,256]{1,0:T(8,128)(2,1)} %g_ref.1), calls=%async_computation.4 | async-start | bytes 131072 | tf_op jit(solution)/shard_map/slice | solution.py:335
  4.8 9.8 %copy-start.6 = (f32[128]{0:T(128)S(1)}, f32[128]{0:T(128)}, u32[]{:S(2)}) copy-start(f32[128]{0:T(128)} %param.21) | copy-start | bytes 1540
  4.8 31.9 %all-to-all-start = ((bf16[8,2,128,512]{3,2,1,0:T(8,128)(2,1)}), bf16[8,2,128,512]{3,2,1,0:T(8,128)(2,1)S(1)}, u32[]{:S(2)}, u32[]{:S(2)}) async-start(bf16[8,2,128,512]{3,2,1,0:T(8,128)(2,1)} %get-tuple-element.24), calls=%async_computation | async-start | bytes 4194304 | tf_op jit(solution)/shard_map/all_to_all | solution.py:332
  10.2 5.3 %collective-permute-start.1 = (bf16[128,1024]{1,0:T(8,128)(2,1)S(1)}, bf16[128,1024]{1,0:T(8,128)(2,1)S(1)}, u32[]{:S(2)}, u32[]{:S(2)}) collective-permute-start(bf16[128,1024]{1,0:T(8,128)(2,1)S(1)} %pad_maximum_fusion), channel_id=1, source_target_pairs={{4,0},{8,4},{12,8},{16,12},{20,16},{24,20},{28,24},{5,1},{9,5},{13... | collective-permute-start | bytes 786440 | tf_op jit(solution)/shard_map/ppermute | solution.py:337
  11.5 4.0 %collective-permute-start = (bf16[128,512]{1,0:T(8,128)(2,1)S(1)}, bf16[128,512]{1,0:T(8,128)(2,1)S(1)}, u32[]{:S(2)}, u32[]{:S(2)}) collective-permute-start(bf16[128,512]{1,0:T(8,128)(2,1)S(1)} %pad_maximum_fusion.1), channel_id=1, source_target_pairs={{0,4},{4,8},{8,12},{12,16},{16,20},{20,24},{24,28},{1,5},{5,9},{9,... | collective-permute-start | bytes 393224 | tf_op jit(solution)/shard_map/ppermute | solution.py:336
  15.5 0.7 copy-start.5
  15.6 0.7 copy-start.2
  36.7 17.8 %copy-start = (bf16[8,2,128,512]{3,2,1,0:T(8,128)(2,1)}, bf16[8,2,128,512]{3,2,1,0:T(8,128)(2,1)S(1)}, u32[]{:S(2)}) copy-start(bf16[8,2,128,512]{3,2,1,0:T(8,128)(2,1)S(1)} %all-to-all-done.refs_0_) | copy-start | bytes 6291460
  36.7 27.7 %all-to-all-start.2 = ((f32[32,1,256]{2,1,0:T(1,128)}), f32[32,1,256]{2,1,0:T(1,128)S(1)}, u32[]{:S(2)}, u32[]{:S(2)}) async-start(f32[32,1,256]{2,1,0:T(1,128)} %copy.21), calls=%async_computation.2 | async-start | bytes 65536 | tf_op jit(solution)/shard_map/all_to_all | solution.py:345
  64.5 30.6 %all-to-all-start.1 = ((bf16[8,2,128,512]{3,2,1,0:T(8,128)(2,1)}), bf16[8,2,128,512]{3,2,1,0:T(8,128)(2,1)S(1)}, u32[]{:S(2)}, u32[]{:S(2)}) async-start(bf16[8,2,128,512]{3,2,1,0:T(8,128)(2,1)} %get-tuple-element.25), calls=%async_computation.1 | async-start | bytes 4194304 | tf_op jit(solution)/shard_map/all_to_all | solution.py:349
  95.0 1.3 %copy-start.1 = (bf16[8,2,128,512]{3,2,1,0:T(8,128)(2,1)}, bf16[8,2,128,512]{3,2,1,0:T(8,128)(2,1)S(1)}, u32[]{:S(2)}) copy-start(bf16[8,2,128,512]{3,2,1,0:T(8,128)(2,1)S(1)} %all-to-all-done.1.home_ref) | copy-start | bytes 6291460
